TPU v7x, 32 devices: a whole 2x2x4 slice. The times are simulated.
32 devices in a mesh: lat: 4 (over y, x), kpt: 8 (over z, core).
Axes of the slice: x: 2, y: 2, z: 4, core: 2. Of those that a mesh axis runs over, the one named last changes fastest.
Arguments:
- coarse: bfloat16 [2, 4, 32, 12288], P(None, 'lat', 'kpt'), may hold values from -1 to 1
- rp_vectors: int32 [4, 3], P('lat'), may hold values from -4 to 4
- rp_weights: int32 [4], P('lat'), may hold values from 1 to 3
- re_vectors: int32 [32, 3], replicated, may hold values from -4 to 4
- re_weights: int32 [32], replicated, may hold values from 1 to 3
- q_points: float32 [2, 3], replicated, may hold values from 0 to 1
- k_points: float32 [512, 3], P('kpt'), may hold values from 0 to 1
- modes_rot: bfloat16 [2, 2, 48, 48], replicated, may hold values from -0.625 to 0.625
- u_k: bfloat16 [2, 512, 16, 16], P(None, 'kpt'), may hold values from -1 to 1
- u_kq: bfloat16 [2, 2, 512, 16, 16], P(None, None, 'kpt'), may hold values from -1 to 1
- mask_k: int32 [512, 16], P('kpt'), may hold values 0 or 1
- mask_kq: int32 [2, 512, 16], P(None, 'kpt'), may hold values 0 or 1
Outputs:
- coupling: bfloat16 [2, 512, 2, 12288], P(None, 'kpt', None, 'lat')
All inputs are finite; a program needn't handle non-finite values. No bound on the sum of `mask_k` or of `mask_kq` on one device may be relied on, other than what follows from the above.
Results may differ from a plain program's by a relative error of at most 0.017.
Values may be sent and summed in bfloat16 or wider, within the bound.
A program may use at most 128 MiB of HBM per device.

v0:
```python
import jax
import jax.numpy as jnp
from jax import lax
from jax.sharding import PartitionSpec as P

two_pi = 6.283185307179586


def phases(points, vectors, weights):
    cells = vectors.astype(jnp.float32)
    argument = two_pi * (
        points[:, 0:1] * cells[None, :, 0]
        + points[:, 1:2] * cells[None, :, 1]
        + points[:, 2:3] * cells[None, :, 2]
    )
    inverse = 1.0 / weights.astype(jnp.float32)
    return (
        (jnp.cos(argument) * inverse).astype(jnp.bfloat16),
        (jnp.sin(argument) * inverse).astype(jnp.bfloat16),
    )


def rotate_modes(values, modes_rot):
    shape = values.shape
    mode_count = modes_rot.shape[2]
    split = values.reshape(shape[0], shape[1], shape[2], mode_count, shape[3] // mode_count)
    br = jnp.einsum(
        "qmn,qrmx->qrnx", modes_rot[0], split[0], preferred_element_type=jnp.float32
    ) - jnp.einsum("qmn,qrmx->qrnx", modes_rot[1], split[1], preferred_element_type=jnp.float32)
    bi = jnp.einsum(
        "qmn,qrmx->qrnx", modes_rot[0], split[1], preferred_element_type=jnp.float32
    ) + jnp.einsum("qmn,qrmx->qrnx", modes_rot[1], split[0], preferred_element_type=jnp.float32)
    return jnp.stack([br, bi]).reshape(shape).astype(jnp.bfloat16)


def phonon_sum(block, vectors, weights, q_points):
    phase_real, phase_imag = phases(q_points, vectors, weights)
    rows = block.shape[1]
    cells = block.shape[2]
    lanes = block.shape[3]
    flat_real = block[0].reshape(rows, cells * lanes)
    flat_imag = block[1].reshape(rows, cells * lanes)
    part_real = jnp.dot(phase_real, flat_real, preferred_element_type=jnp.float32) - jnp.dot(
        phase_imag, flat_imag, preferred_element_type=jnp.float32
    )
    part_imag = jnp.dot(phase_real, flat_imag, preferred_element_type=jnp.float32) + jnp.dot(
        phase_imag, flat_real, preferred_element_type=jnp.float32
    )
    return jnp.stack([part_real, part_imag]).reshape(2, q_points.shape[0], cells, lanes)


def per_device(
    coarse,
    rp_vectors,
    rp_weights,
    re_vectors,
    re_weights,
    q_points,
    k_points,
    modes_rot,
    u_k,
    u_kq,
    mask_k,
    mask_kq,
):
    q_count = q_points.shape[0]
    k_count = k_points.shape[0]
    band_count = u_k.shape[2]
    all_vectors, all_weights = (
        lax.all_gather(rp_vectors, "lat", axis=0, tiled=True),
        lax.all_gather(rp_weights, "lat", axis=0, tiled=True),
    )
    blocks = lax.all_to_all(coarse, "lat", split_axis=2, concat_axis=1, tiled=True)
    summed = phonon_sum(blocks, all_vectors, all_weights, q_points).astype(jnp.bfloat16)
    rotated = rotate_modes(summed, modes_rot)
    shared = lax.all_to_all(rotated, "lat", split_axis=3, concat_axis=2, tiled=True)
    lane_local = shared.shape[3]
    portion = lax.all_gather(shared, "kpt", axis=2, tiled=True)
    kreal, kimag = phases(k_points, re_vectors, re_weights)
    er = jnp.einsum(
        "kr,qrx->kqx", kreal, portion[0], preferred_element_type=jnp.float32
    ) - jnp.einsum("kr,qrx->kqx", kimag, portion[1], preferred_element_type=jnp.float32)
    ei = jnp.einsum(
        "kr,qrx->kqx", kreal, portion[1], preferred_element_type=jnp.float32
    ) + jnp.einsum("kr,qrx->kqx", kimag, portion[0], preferred_element_type=jnp.float32)
    totals = jnp.stack([er, ei])
    mode_local = lane_local // (band_count * band_count)
    field = totals.astype(jnp.bfloat16).reshape(
        2, k_count, q_count, mode_local, band_count, band_count
    )
    tr = jnp.einsum(
        "kqmab,kbn->kqman", field[0], u_k[0], preferred_element_type=jnp.float32
    ) - jnp.einsum("kqmab,kbn->kqman", field[1], u_k[1], preferred_element_type=jnp.float32)
    ti = jnp.einsum(
        "kqmab,kbn->kqman", field[0], u_k[1], preferred_element_type=jnp.float32
    ) + jnp.einsum("kqmab,kbn->kqman", field[1], u_k[0], preferred_element_type=jnp.float32)
    tr = tr.astype(jnp.bfloat16)
    ti = ti.astype(jnp.bfloat16)
    outr = jnp.einsum(
        "qkac,kqman->kqmcn", u_kq[0], tr, preferred_element_type=jnp.float32
    ) + jnp.einsum("qkac,kqman->kqmcn", u_kq[1], ti, preferred_element_type=jnp.float32)
    outi = jnp.einsum(
        "qkac,kqman->kqmcn", u_kq[0], ti, preferred_element_type=jnp.float32
    ) - jnp.einsum("qkac,kqman->kqmcn", u_kq[1], tr, preferred_element_type=jnp.float32)
    window = (
        jnp.transpose(mask_kq.astype(jnp.float32), (1, 0, 2))[:, :, None, :, None]
        * mask_k.astype(jnp.float32)[:, None, None, None, :]
    )
    result = jnp.stack([outr * window, outi * window])
    return result.reshape(2, k_count, q_count, lane_local).astype(jnp.bfloat16)


def solution(mesh):
    placed = (
        P(None, "lat", "kpt", None),
        P("lat", None),
        P("lat"),
        P(),
        P(),
        P(),
        P("kpt", None),
        P(),
        P(None, "kpt", None, None),
        P(None, None, "kpt", None, None),
        P("kpt", None),
        P(None, "kpt", None),
    )
    return jax.shard_map(
        per_device,
        mesh=mesh,
        in_specs=placed,
        out_specs=P(None, "kpt", None, "lat"),
        check_vma=False,
    )
```

profile of v0, /device:TPU:0, one launch (start us, length us, event | category | flops | bytes accessed | tf_op | source)
XLA Modules:
  0.0 252.8 jit_solution(12334398810767427954)
XLA Ops:
  0.7 1.8 copy.132
  2.5 1.2 dynamic-slice
  3.7 0.7 dynamic-update-slice
  4.4 5.2 %all-to-all-start = ((bf16[2,1,4,12288]{3,0,1,2:T(2,128)(2,1)}), bf16[2,1,4,12288]{3,0,1,2:T(2,128)(2,1)S(1)}, u32[]{:S(2)}, u32[]{:S(2)}) async-start(bf16[2,1,4,12288]{3,0,1,2:T(2,128)(2,1)} %copy.132), calls=%async_computation | async-start | bytes 393216 | tf_op jit(solution)/shard_map/all_to_all | solution.py:73
  9.6 7.9 %all-reduce = s32[4]{0:T(128)S(1)} all-reduce(s32[4]{0:T(128)S(1)} %dynamic-update-slice), channel_id=1, replica_groups=mesh['lat'=4,'kpt'=8] {'lat'}, use_global_device_ids=true, to_apply=%add | all-reduce | flops 4 | bytes 32
  17.5 1.0 slice_reduce_fusion.5
  18.5 0.8 slice_bitcast_fusion.5
  19.3 7.8 %all-gather = s32[4,1,3]{2,1,0:T(1,128)S(1)} all-gather(s32[1,1,3]{2,1,0:T(1,128)} %bitcast.155), channel_id=1, replica_groups=mesh['lat'=4,'kpt'=8] {'lat'}, dimensions={0}, use_global_device_ids=true | all-gather | bytes 60 | tf_op jit(solution)/shard_map/all_gather | solution.py:70
  27.1 0.2 slice_reduce_fusion.2
  27.3 0.7 convert_element_type.56
  28.0 0.7 convert_element_type.67
  28.7 0.7 convert_bitcast_fusion
  29.4 0.9 fusion.67
  30.3 1.0 fusion.65
  31.3 0.7 broadcast_multiply_fusion
  32.0 0.1 add_multiply_fusion.1
  32.1 0.0 all-to-all-done
  32.1 0.3 fusion.66
  32.4 0.3 fusion.30
  32.7 0.3 fusion.26
  32.9 0.3 fusion
  33.2 0.3 fusion.1
  33.4 0.9 fusion.35
  34.3 0.9 fusion.33
  35.3 0.9 fusion.9
  36.2 0.9 fusion.8
  37.1 0.1 pad_maximum_fusion.1
  37.3 0.0 copy-start.3
  37.3 10.0 %copy.135 = bf16[2,2,1,12288]{1,0,2,3:T(2,128)(2,1)} copy(bf16[2,2,1,12288]{3,1,2,0:T(2,128)(2,1)S(1)} %pad_maximum_fusion.1) | data formatting | bytes 196608 | tf_op jit(solution)/shard_map/stack | solution.py:33
  47.3 11.9 %reshape.167 = bf16[4,2,6144]{2,1,0:T(2,128)(2,1)} reshape(bf16[12288,1,2,2]{3,2,1,0:T(2,128)(2,1)} %bitcast.144) | data formatting | bytes 196608
  59.3 3.3 %all-to-all-start.1 = ((bf16[4,2,6144]{2,1,0:T(2,128)(2,1)}), bf16[4,2,6144]{2,1,0:T(2,128)(2,1)S(1)}, u32[]{:S(2)}, u32[]{:S(2)}) async-start(bf16[4,2,6144]{2,1,0:T(2,128)(2,1)} %reshape.167), calls=%async_computation.1 | async-start | bytes 196608 | tf_op jit(solution)/shard_map/all_to_all | solution.py:76
  62.6 0.0 copy-done.3
  62.6 0.3 copy.175
  62.9 0.9 copy.176
  63.8 0.8 copy.178
  64.6 0.8 copy.177
  65.4 2.1 all-to-all-done.1
  67.5 14.7 %reshape.168 = bf16[12288,1,2,2]{3,2,1,0:T(2,128)(2,1)} reshape(bf16[4,2,6144]{2,1,0:T(2,128)(2,1)S(1)} %all-to-all-done.1) | data formatting | bytes 196608
  82.2 12.7 %copy.137 = bf16[2,2,4,3072]{3,1,0,2:T(2,128)(2,1)S(1)} copy(bf16[2,2,4,3072]{1,0,3,2:T(2,128)(2,1)} %bitcast.145) | data formatting | bytes 196608 | tf_op jit(solution)/shard_map/all_to_all | solution.py:76
  94.8 16.5 %all_gather.11 = bf16[2,2,32,3072]{3,1,0,2:T(2,128)(2,1)S(1)} all-gather(bf16[2,2,4,3072]{3,1,0,2:T(2,128)(2,1)S(1)} %copy.137), channel_id=1, replica_groups=mesh['lat'=4,'kpt'=8] {'kpt'}, dimensions={2}, use_global_device_ids=true | all-gather | bytes 884736 | tf_op jit(solution)/shard_map/all_gather | solution.py:78
  111.3 0.5 fusion.64
  111.8 0.5 fusion.19
  112.4 0.5 fusion.18
  112.9 1.4 fusion.3
  114.4 2.4 copy.143
  116.8 1.4 fusion.2
  118.2 1.8 copy.140
  120.0 9.8 %copy.142 = bf16[64,2,12,16,16]{4,3,2,1,0:T(8,128)(2,1)} copy(bf16[64,2,12,16,16]{0,4,3,2,1:T(8,128)(2,1)S(1)} %bitcast.147) | data formatting | bytes 1572864 | tf_op jit(solution)/shard_map/squeeze | solution.py:92
  129.8 10.8 %copy.145 = bf16[64,2,12,16,16]{4,3,2,1,0:T(8,128)(2,1)} copy(bf16[64,2,12,16,16]{0,4,3,2,1:T(8,128)(2,1)} %bitcast.146) | data formatting | bytes 1572864 | tf_op jit(solution)/shard_map/squeeze | solution.py:93
  140.6 9.2 %fusion.23 = f32[64,2,12,16,16]{4,3,2,1,0:T(8,128)} fusion(bf16[64,2,12,16,16]{4,3,2,1,0:T(8,128)(2,1)} %copy.142, bf16[1,64,16,16]{3,2,1,0:T(8,128)(2,1)} %copy.176), kind=kOutput, calls=%fused_computation.36 | convolution fusion | flops 12582912 | bytes 2392064 | tf_op jit(solution)/shard_map/kqmab,kbn->kqman/dot_general | solution.py:94
  149.8 5.5 %fusion.21 = f32[64,2,12,16,16]{4,3,2,1,0:T(8,128)} fusion(bf16[64,2,12,16,16]{4,3,2,1,0:T(8,128)(2,1)S(1)} %bitcast.143, bf16[1,64,16,16]{3,2,1,0:T(8,128)(2,1)S(1)} %copy.175), kind=kOutput, calls=%fused_computation.34 | convolution fusion | flops 12582912 | bytes 2392064 | tf_op jit(solution)/shard_map/kqmab,kbn->kqman/dot_general | solution.py:91
  155.3 8.2 %add_convert_fusion = bf16[64,2,12,16,16]{4,3,2,1,0:T(8,128)(2,1)S(1)} fusion(f32[64,2,12,16,16]{4,3,2,1,0:T(8,128)} %fusion.23, bf16[64,2,12,16,16]{4,3,2,1,0:T(8,128)(2,1)} %copy.145, bf16[1,64,16,16]{3,2,1,0:T(8,128)(2,1)S(1)} %copy.175), kind=kOutput, calls=%fused_computation.4 | convolution fusion | flops 13369344 | bytes 3178496 | tf_op jit(solution)/shard_map/kqmab,kbn->kqman/dot_general | solution.py:96
  163.5 10.9 %subtract_convert_fusion = bf16[64,2,12,16,16]{4,3,2,1,0:T(8,128)(2,1)} fusion(f32[64,2,12,16,16]{4,3,2,1,0:T(8,128)} %fusion.21, bf16[64,2,12,16,16]{4,3,2,1,0:T(8,128)(2,1)} %copy.145, bf16[1,64,16,16]{3,2,1,0:T(8,128)(2,1)S(1)} %copy-done.1), kind=kOutput, calls=%fused_computation.5 | convolution fusion | flops 13369344 | bytes 3178496 | tf_op jit(solution)/shard_map/kqmab,kbn->kqman/dot_general | solution.py:93
  174.4 9.7 %fusion.10 = f32[64,2,12,16,16]{4,3,2,1,0:T(8,128)} fusion(bf16[64,2,12,16,16]{4,3,2,1,0:T(8,128)(2,1)} %subtract_convert_fusion, bf16[1,2,64,16,16]{4,3,1,2,0:T(8,128)(2,1)S(1)} %copy.178), kind=kOutput, calls=%fused_computation.21 | convolution fusion | flops 12582912 | bytes 2424832 | tf_op jit(solution)/shard_map/qkac,kqman->kqmcn/dot_general | solution.py:104
  184.1 5.7 %fusion.16 = f32[64,2,12,16,16]{4,3,2,1,0:T(8,128)} fusion(bf16[64,2,12,16,16]{4,3,2,1,0:T(8,128)(2,1)S(1)} %copy-done, bf16[1,2,64,16,16]{4,3,1,2,0:T(8,128)(2,1)S(1)} %copy.177), kind=kOutput, calls=%fused_computation.27 | convolution fusion | flops 12582912 | bytes 2424832 | tf_op jit(solution)/shard_map/qkac,kqman->kqmcn/dot_general | solution.py:99
  189.8 5.6 %fusion.14 = f32[64,2,12,16,16]{4,3,2,1,0:T(8,128)} fusion(bf16[64,2,12,16,16]{4,3,2,1,0:T(8,128)(2,1)S(1)} %add_convert_fusion, bf16[1,2,64,16,16]{4,3,1,2,0:T(8,128)(2,1)S(1)} %copy.177), kind=kOutput, calls=%fused_computation.25 | convolution fusion | flops 12582912 | bytes 2424832 | tf_op jit(solution)/shard_map/qkac,kqman->kqmcn/dot_general | solution.py:102
  195.5 5.8 %fusion.12 = f32[64,2,12,16,16]{4,3,2,1,0:T(8,128)} fusion(bf16[64,2,12,16,16]{4,3,2,1,0:T(8,128)(2,1)S(1)} %add_convert_fusion, bf16[1,2,64,16,16]{4,3,1,2,0:T(8,128)(2,1)S(1)} %copy.178), kind=kOutput, calls=%fused_computation.23 | convolution fusion | flops 12582912 | bytes 2424832 | tf_op jit(solution)/shard_map/qkac,kqman->kqmcn/dot_general | solution.py:101
  201.3 9.7 %copy.157 = f32[64,2,12,16,16]{0,3,4,2,1:T(8,128)S(1)} copy(f32[64,2,12,16,16]{4,3,2,1,0:T(8,128)} %fusion.10) | data formatting | bytes 3145728 | tf_op jit(solution)/shard_map/qkac,kqman->kqmcn/dot_general | solution.py:104
  211.0 10.9 %copy.152 = f32[64,2,12,16,16]{0,3,4,2,1:T(8,128)} copy(f32[64,2,12,16,16]{4,3,2,1,0:T(8,128)} %fusion.16) | data formatting | bytes 3145728 | tf_op jit(solution)/shard_map/qkac,kqman->kqmcn/dot_general | solution.py:99
  221.9 10.9 %copy.156 = f32[64,2,12,16,16]{0,3,4,2,1:T(8,128)} copy(f32[64,2,12,16,16]{4,3,2,1,0:T(8,128)} %fusion.14) | data formatting | bytes 3145728 | tf_op jit(solution)/shard_map/qkac,kqman->kqmcn/dot_general | solution.py:102
  232.8 10.9 %copy.153 = f32[64,2,12,16,16]{0,3,4,2,1:T(8,128)} copy(f32[64,2,12,16,16]{4,3,2,1,0:T(8,128)} %fusion.12) | data formatting | bytes 3145728 | tf_op jit(solution)/shard_map/qkac,kqman->kqmcn/dot_general | solution.py:101
  243.7 5.0 %fusion.5 = (bf16[64,2,12,16,16]{0,4,3,2,1:T(8,128)(2,1)S(1)}, bf16[64,2,12,16,16]{0,4,3,2,1:T(8,128)(2,1)S(1)}) fusion(f32[64,2,12,16,16]{0,3,4,2,1:T(8,128)} %copy.152, f32[64,2,12,16,16]{0,3,4,2,1:T(8,128)} %copy.153, f32[64,2,16,16]{0,3,2,1:T(8,128)S(1)} %copy-done.2, f32[64,2,12,16,16]{0,3,4,2,1:T(8,128)} %copy.156, f32[64,2,12,16,16]{0,3,4,2,1:T(8,128)S(1)} %copy.157), kind=kLoop, calls=%fused_computation.14 | loop fusion | flops 2359296 | bytes 7995392 | tf_op jit(solution)/shard_map/convert.3
  248.8 0.7 pad_maximum_fusion
  249.5 3.3 %copy.158 = bf16[2,64,2,3072]{3,2,1,0:T(2,128)(2,1)} copy(bf16[2,64,2,3072]{1,3,2,0:T(8,128)(2,1)S(1)} %pad_maximum_fusion) | data formatting | bytes 3145728 | tf_op jit(solution)/shard_map/stack | solution.py:109
  (18 shorter events, 0.1 us)
Async XLA Ops:
  4.4 27.8 %all-to-all-start = ((bf16[2,1,4,12288]{3,0,1,2:T(2,128)(2,1)}), bf16[2,1,4,12288]{3,0,1,2:T(2,128)(2,1)S(1)}, u32[]{:S(2)}, u32[]{:S(2)}) async-start(bf16[2,1,4,12288]{3,0,1,2:T(2,128)(2,1)} %copy.132), calls=%async_computation | async-start | bytes 393216 | tf_op jit(solution)/shard_map/all_to_all | solution.py:73
  37.3 25.3 %copy-start.3 = (s32[32]{0:T(128)S(1)}, s32[32]{0:T(128)}, u32[]{:S(2)}) copy-start(s32[32]{0:T(128)} %param.16) | copy-start | bytes 388
  59.3 8.2 %all-to-all-start.1 = ((bf16[4,2,6144]{2,1,0:T(2,128)(2,1)}), bf16[4,2,6144]{2,1,0:T(2,128)(2,1)S(1)}, u32[]{:S(2)}, u32[]{:S(2)}) async-start(bf16[4,2,6144]{2,1,0:T(2,128)(2,1)} %reshape.167), calls=%async_computation.1 | async-start | bytes 196608 | tf_op jit(solution)/shard_map/all_to_all | solution.py:76
  129.8 20.0 %slice-start = ((s8[6291456]{0:T(1024)(128)(4,1)}), s8[2097152]{0:T(1024)(128)(4,1)S(1)}, s32[]{:S(2)}) async-start(s8[6291456]{0:T(1024)(128)(4,1)} %bitcast.142), calls=%async_computation.2 | async-start | bytes 4194304
  140.6 9.2 %slice-start.1 = ((s8[6291456]{0:T(1024)(128)(4,1)}), s8[4194304]{0:T(1024)(128)(4,1)S(1)}, s32[]{:S(2)}) async-start(s8[6291456]{0:T(1024)(128)(4,1)} %bitcast.142), calls=%async_computation.3 | async-start | bytes 8388608
  155.3 8.2 %copy-start.1 = (bf16[1,64,16,16]{3,2,1,0:T(8,128)(2,1)S(1)}, bf16[1,64,16,16]{3,2,1,0:T(8,128)(2,1)}, u32[]{:S(2)}) copy-start(bf16[1,64,16,16]{3,2,1,0:T(8,128)(2,1)} %copy.176) | copy-start | bytes 98308
  174.4 9.7 %copy-start = (bf16[64,2,12,16,16]{4,3,2,1,0:T(8,128)(2,1)S(1)}, bf16[64,2,12,16,16]{4,3,2,1,0:T(8,128)(2,1)}, u32[]{:S(2)}) copy-start(bf16[64,2,12,16,16]{4,3,2,1,0:T(8,128)(2,1)} %subtract_convert_fusion) | copy-start | bytes 2359300
  232.8 10.9 %copy-start.2 = (f32[64,2,16,16]{0,3,2,1:T(8,128)S(1)}, f32[64,2,16,16]{0,3,2,1:T(8,128)}, u32[]{:S(2)}) copy-start(f32[64,2,16,16]{0,3,2,1:T(8,128)} %broadcast_multiply_fusion) | copy-start | bytes 393220
where the time goes:
time: 254 us; the launch traced here: 253 us
  local copies, waits for them, and re-layouts  131 us (52%)
  matrix products  69.2 us (27%)
  blocking collectives  32.2 us (13%)
  other arithmetic  8.81 us (3%)
  starting transfers between devices  8.5 us (3%)
    unnamed x22, local copies, waits for them, and re-layouts  33.1 us
    all_gather x1, blocking collectives, per_device(): portion = lax.all_gather(shared, 'kpt', axis=2, tiled=True)  16.5 us
    all_to_all x1, local copies, waits for them, and re-layouts, per_device(): lax.all_to_all(rotated, 'lat', split_axis=3, concat_axis=2, tiled=True)  12.7 us
    dot_general x1, local copies, waits for them, and re-layouts, per_device(): jnp.einsum('qkac,kqman->kqmcn', u_kq[1], ti, preferred_element_type=jnp.f...  10.9 us
    dot_general x1, local copies, waits for them, and re-layouts, per_device(): jnp.einsum('qkac,kqman->kqmcn', u_kq[0], tr, preferred_element_type=jnp.f...  10.9 us
    dot_general x1, local copies, waits for them, and re-layouts, per_device(): jnp.einsum('qkac,kqman->kqmcn', u_kq[0], ti, preferred_element_type=jnp.f...  10.9 us
    dot_general x1, matrix products, per_device(): jnp.einsum('kqmab,kbn->kqman', field[1], u_k[1], preferred_element_type=j...  10.9 us
    squeeze x1, local copies, waits for them, and re-layouts, per_device(): field[1]  10.8 us
  transfers between devices with their start and end apart: 2, of which 1 were waited for; matrix products, arithmetic and copies ran while one was open for 4% of the time, Pallas kernels for 0%

commit v1 on v0

--- a/solution.py
+++ b/solution.py
@@ -73,7 +73,10 @@
     blocks = lax.all_to_all(coarse, "lat", split_axis=2, concat_axis=1, tiled=True)
     summed = phonon_sum(blocks, all_vectors, all_weights, q_points).astype(jnp.bfloat16)
     rotated = rotate_modes(summed, modes_rot)
-    shared = lax.all_to_all(rotated, "lat", split_axis=3, concat_axis=2, tiled=True)
+    n_dev = lax.axis_size("lat")
+    pieces = jnp.stack(jnp.split(rotated, n_dev, axis=3), axis=0)
+    pieces = lax.all_to_all(pieces, "lat", split_axis=0, concat_axis=0)
+    shared = jnp.concatenate(pieces, axis=2)
     lane_local = shared.shape[3]
     portion = lax.all_gather(shared, "kpt", axis=2, tiled=True)
     kreal, kimag = phases(k_points, re_vectors, re_weights)

time: 254 us -> 206 us (0.81)
  local copies, waits for them, and re-layouts: 131 us -> 81.7 us
    unnamed x22 -> x18, local copies, waits for them, and re-layouts: 33.1 us -> 6.49 us
    all_to_all x1 -> x0, local copies, waits for them, and re-layouts: 12.7 us -> none  [per_device(): lax.all_to_all(rotated, 'lat', split_axis=3, concat_axis=2, tiled=True)]
    another operation x3 -> x2, local copies, waits for them, and re-layouts: 10 us -> 0.04 us  [rotate_modes(): return jnp.stack([br, bi]).reshape(shape).astype(jnp.bfloat16)]
    another operation x2 -> x3, other arithmetic: 5.19 us -> 5.95 us
  transfers between devices with their start and end apart: 2 -> 2, of which waited for: 1 -> 1; matrix products, arithmetic and copies ran while one was open for 4% -> 5% of each run, Pallas kernels for 0% -> 0%
where the time goes in v1:
time: 206 us; the launch traced here: 204 us
  local copies, waits for them, and re-layouts  81.7 us (40%)
  matrix products  69.2 us (34%)
  blocking collectives  32.2 us (16%)
  other arithmetic  10.2 us (5%)
  starting transfers between devices  8.5 us (4%)
    all_gather x1, blocking collectives, per_device(): portion = lax.all_gather(shared, 'kpt', axis=2, tiled=True)  16.5 us
    dot_general x1, local copies, waits for them, and re-layouts, per_device(): jnp.einsum('qkac,kqman->kqmcn', u_kq[1], ti, preferred_element_type=jnp.f...  10.9 us
    dot_general x1, local copies, waits for them, and re-layouts, per_device(): jnp.einsum('qkac,kqman->kqmcn', u_kq[0], tr, preferred_element_type=jnp.f...  10.9 us
    dot_general x1, local copies, waits for them, and re-layouts, per_device(): jnp.einsum('qkac,kqman->kqmcn', u_kq[0], ti, preferred_element_type=jnp.f...  10.9 us
    dot_general x1, matrix products, per_device(): jnp.einsum('kqmab,kbn->kqman', field[1], u_k[1], preferred_element_type=j...  10.9 us
    squeeze x1, local copies, waits for them, and re-layouts, per_device(): field[1]  10.8 us
    squeeze x1, local copies, waits for them, and re-layouts, per_device(): field[0]  9.81 us
    dot_general x1, matrix products, per_device(): jnp.einsum('qkac,kqman->kqmcn', u_kq[1], tr, preferred_element_type=jnp.f...  9.73 us
  transfers between devices with their start and end apart: 2, of which 1 were waited for; matrix products, arithmetic and copies ran while one was open for 5% of the time, Pallas kernels for 0%

profile of v1, /device:TPU:0, one launch (start us, length us, event | category | flops | bytes accessed | tf_op | source)
XLA Modules:
  0.0 204.2 jit_solution(2790608858082249442)
XLA Ops:
  0.7 1.8 copy.220
  2.5 1.2 dynamic-slice
  3.7 0.7 dynamic-update-slice
  4.4 5.2 %all-to-all-start = ((bf16[2,1,4,12288]{3,0,1,2:T(2,128)(2,1)}), bf16[2,1,4,12288]{3,0,1,2:T(2,128)(2,1)S(1)}, u32[]{:S(2)}, u32[]{:S(2)}) async-start(bf16[2,1,4,12288]{3,0,1,2:T(2,128)(2,1)} %copy.220), calls=%async_computation | async-start | bytes 393216 | tf_op jit(solution)/shard_map/all_to_all | solution.py:73
  9.6 7.9 %all-reduce = s32[4]{0:T(128)S(1)} all-reduce(s32[4]{0:T(128)S(1)} %dynamic-update-slice), channel_id=1, replica_groups=mesh['lat'=4,'kpt'=8] {'lat'}, use_global_device_ids=true, to_apply=%add | all-reduce | flops 4 | bytes 32
  17.5 1.0 slice_reduce_fusion.5
  18.5 0.8 slice_bitcast_fusion.5
  19.3 7.8 %all-gather.1 = s32[4,1,3]{2,1,0:T(1,128)S(1)} all-gather(s32[1,1,3]{2,1,0:T(1,128)} %bitcast.166), channel_id=1, replica_groups=mesh['lat'=4,'kpt'=8] {'lat'}, dimensions={0}, use_global_device_ids=true | all-gather | bytes 60 | tf_op jit(solution)/shard_map/all_gather | solution.py:70
  27.1 0.2 slice_reduce_fusion.2
  27.3 0.7 convert_element_type.56
  28.0 0.7 convert_element_type.67
  28.7 0.7 convert_bitcast_fusion
  29.4 0.9 fusion.74
  30.3 1.0 fusion.72
  31.3 0.7 broadcast_multiply_fusion
  32.0 0.1 add_multiply_fusion.1
  32.1 0.0 all-to-all-done
  32.1 0.3 fusion.73
  32.4 0.3 fusion.30
  32.7 0.3 fusion.26
  32.9 0.3 fusion
  33.2 0.3 fusion.1
  33.4 0.9 fusion.35
  34.3 0.9 fusion.33
  35.3 0.9 fusion.9
  36.2 0.9 fusion.8
  37.1 0.1 fusion.55
  37.2 0.8 maximum_bitcast_fusion
  38.1 3.3 %all-to-all-start.1 = ((bf16[4,2,2,1,3072]{4,2,3,1,0:T(2,128)(2,1)}), bf16[4,2,2,1,3072]{4,2,3,1,0:T(2,128)(2,1)S(1)}, u32[]{:S(2)}, u32[]{:S(2)}) async-start(bf16[4,2,2,1,3072]{4,2,3,1,0:T(2,128)(2,1)} %maximum_bitcast_fusion), calls=%async_computation.1 | async-start | bytes 196608 | tf_op jit(solution)/shard_map/all_to_all | solution.py:78
  41.4 0.7 convert_divide_fusion.1
  42.0 0.3 copy.261
  42.3 0.9 copy.262
  43.2 0.8 copy.264
  44.0 0.8 copy.263
  44.8 1.5 all-to-all-done.1
  46.3 16.5 %all-gather = bf16[2,2,32,1,3072]{4,1,3,0,2:T(2,128)(2,1)S(1)} all-gather(bf16[2,2,4,1,3072]{4,1,3,0,2:T(2,128)(2,1)S(1)} %bitcast.158), channel_id=2, replica_groups=mesh['lat'=4,'kpt'=8] {'kpt'}, dimensions={2}, use_global_device_ids=true | all-gather | bytes 884736 | tf_op jit(solution)/shard_map/all_gather | solution.py:81
  62.7 0.5 fusion.71
  63.3 0.5 fusion.19
  63.8 0.5 fusion.18
  64.4 1.4 fusion.3
  65.8 2.4 %copy.231 = bf16[64,2,3072]{0,2,1:T(8,128)(2,1)} copy(bf16[64,2,3072]{2,0,1:T(8,128)(2,1)} %fusion.3) | data formatting | bytes 1572864 | tf_op jit(solution)/shard_map/convert.6
  68.2 1.4 fusion.2
  69.7 1.8 copy.228
  71.4 9.8 %copy.230 = bf16[64,2,12,16,16]{4,3,2,1,0:T(8,128)(2,1)} copy(bf16[64,2,12,16,16]{0,4,3,2,1:T(8,128)(2,1)S(1)} %bitcast.155) | data formatting | bytes 1572864 | tf_op jit(solution)/shard_map/squeeze | solution.py:95
  81.3 10.8 %copy.233 = bf16[64,2,12,16,16]{4,3,2,1,0:T(8,128)(2,1)} copy(bf16[64,2,12,16,16]{0,4,3,2,1:T(8,128)(2,1)} %bitcast.154) | data formatting | bytes 1572864 | tf_op jit(solution)/shard_map/squeeze | solution.py:96
  92.0 9.2 %fusion.23 = f32[64,2,12,16,16]{4,3,2,1,0:T(8,128)} fusion(bf16[64,2,12,16,16]{4,3,2,1,0:T(8,128)(2,1)} %copy.230, bf16[1,64,16,16]{3,2,1,0:T(8,128)(2,1)} %copy.262), kind=kOutput, calls=%fused_computation.36 | convolution fusion | flops 12582912 | bytes 2392064 | tf_op jit(solution)/shard_map/kqmab,kbn->kqman/dot_general | solution.py:97
  101.2 0.0 slice-done
  101.2 0.0 slice-done.1
  101.2 5.5 %fusion.21 = f32[64,2,12,16,16]{4,3,2,1,0:T(8,128)} fusion(bf16[64,2,12,16,16]{4,3,2,1,0:T(8,128)(2,1)S(1)} %bitcast.153, bf16[1,64,16,16]{3,2,1,0:T(8,128)(2,1)S(1)} %copy.261), kind=kOutput, calls=%fused_computation.34 | convolution fusion | flops 12582912 | bytes 2392064 | tf_op jit(solution)/shard_map/kqmab,kbn->kqman/dot_general | solution.py:94
  106.7 8.2 %add_convert_fusion = bf16[64,2,12,16,16]{4,3,2,1,0:T(8,128)(2,1)S(1)} fusion(f32[64,2,12,16,16]{4,3,2,1,0:T(8,128)} %fusion.23, bf16[64,2,12,16,16]{4,3,2,1,0:T(8,128)(2,1)} %copy.233, bf16[1,64,16,16]{3,2,1,0:T(8,128)(2,1)S(1)} %copy.261), kind=kOutput, calls=%fused_computation.4 | convolution fusion | flops 13369344 | bytes 3178496 | tf_op jit(solution)/shard_map/kqmab,kbn->kqman/dot_general | solution.py:99
  114.9 0.0 copy-done.1
  115.0 10.9 %subtract_convert_fusion = bf16[64,2,12,16,16]{4,3,2,1,0:T(8,128)(2,1)} fusion(f32[64,2,12,16,16]{4,3,2,1,0:T(8,128)} %fusion.21, bf16[64,2,12,16,16]{4,3,2,1,0:T(8,128)(2,1)} %copy.233, bf16[1,64,16,16]{3,2,1,0:T(8,128)(2,1)S(1)} %copy-done.1), kind=kOutput, calls=%fused_computation.5 | convolution fusion | flops 13369344 | bytes 3178496 | tf_op jit(solution)/shard_map/kqmab,kbn->kqman/dot_general | solution.py:96
  125.8 9.7 %fusion.10 = f32[64,2,12,16,16]{4,3,2,1,0:T(8,128)} fusion(bf16[64,2,12,16,16]{4,3,2,1,0:T(8,128)(2,1)} %subtract_convert_fusion, bf16[1,2,64,16,16]{4,3,1,2,0:T(8,128)(2,1)S(1)} %copy.264), kind=kOutput, calls=%fused_computation.21 | convolution fusion | flops 12582912 | bytes 2424832 | tf_op jit(solution)/shard_map/qkac,kqman->kqmcn/dot_general | solution.py:107
  135.6 0.0 copy-done
  135.6 5.7 %fusion.16 = f32[64,2,12,16,16]{4,3,2,1,0:T(8,128)} fusion(bf16[64,2,12,16,16]{4,3,2,1,0:T(8,128)(2,1)S(1)} %copy-done, bf16[1,2,64,16,16]{4,3,1,2,0:T(8,128)(2,1)S(1)} %copy.263), kind=kOutput, calls=%fused_computation.27 | convolution fusion | flops 12582912 | bytes 2424832 | tf_op jit(solution)/shard_map/qkac,kqman->kqmcn/dot_general | solution.py:102
  141.3 5.6 %fusion.14 = f32[64,2,12,16,16]{4,3,2,1,0:T(8,128)} fusion(bf16[64,2,12,16,16]{4,3,2,1,0:T(8,128)(2,1)S(1)} %add_convert_fusion, bf16[1,2,64,16,16]{4,3,1,2,0:T(8,128)(2,1)S(1)} %copy.263), kind=kOutput, calls=%fused_computation.25 | convolution fusion | flops 12582912 | bytes 2424832 | tf_op jit(solution)/shard_map/qkac,kqman->kqmcn/dot_general | solution.py:105
  146.9 5.8 %fusion.12 = f32[64,2,12,16,16]{4,3,2,1,0:T(8,128)} fusion(bf16[64,2,12,16,16]{4,3,2,1,0:T(8,128)(2,1)S(1)} %add_convert_fusion, bf16[1,2,64,16,16]{4,3,1,2,0:T(8,128)(2,1)S(1)} %copy.264), kind=kOutput, calls=%fused_computation.23 | convolution fusion | flops 12582912 | bytes 2424832 | tf_op jit(solution)/shard_map/qkac,kqman->kqmcn/dot_general | solution.py:104
  152.7 9.7 %copy.245 = f32[64,2,12,16,16]{0,3,4,2,1:T(8,128)S(1)} copy(f32[64,2,12,16,16]{4,3,2,1,0:T(8,128)} %fusion.10) | data formatting | bytes 3145728 | tf_op jit(solution)/shard_map/qkac,kqman->kqmcn/dot_general | solution.py:107
  162.4 10.9 %copy.240 = f32[64,2,12,16,16]{0,3,4,2,1:T(8,128)} copy(f32[64,2,12,16,16]{4,3,2,1,0:T(8,128)} %fusion.16) | data formatting | bytes 3145728 | tf_op jit(solution)/shard_map/qkac,kqman->kqmcn/dot_general | solution.py:102
  173.3 10.9 %copy.244 = f32[64,2,12,16,16]{0,3,4,2,1:T(8,128)} copy(f32[64,2,12,16,16]{4,3,2,1,0:T(8,128)} %fusion.14) | data formatting | bytes 3145728 | tf_op jit(solution)/shard_map/qkac,kqman->kqmcn/dot_general | solution.py:105
  184.2 10.9 %copy.241 = f32[64,2,12,16,16]{0,3,4,2,1:T(8,128)} copy(f32[64,2,12,16,16]{4,3,2,1,0:T(8,128)} %fusion.12) | data formatting | bytes 3145728 | tf_op jit(solution)/shard_map/qkac,kqman->kqmcn/dot_general | solution.py:104
  195.1 5.0 %fusion.5 = (bf16[64,2,12,16,16]{0,4,3,2,1:T(8,128)(2,1)S(1)}, bf16[64,2,12,16,16]{0,4,3,2,1:T(8,128)(2,1)S(1)}) fusion(f32[64,2,12,16,16]{0,3,4,2,1:T(8,128)} %copy.240, f32[64,2,12,16,16]{0,3,4,2,1:T(8,128)} %copy.241, f32[64,2,16,16]{0,3,2,1:T(8,128)S(1)} %copy-done.2, f32[64,2,12,16,16]{0,3,4,2,1:T(8,128)} %copy.244, f32[64,2,12,16,16]{0,3,4,2,1:T(8,128)S(1)} %copy.245), kind=kLoop, calls=%fused_computation.14 | loop fusion | flops 2359296 | bytes 7995392 | tf_op jit(solution)/shard_map/convert.3
  200.2 0.7 pad_maximum_fusion
  200.9 3.3 %copy.246 = bf16[2,64,2,3072]{3,2,1,0:T(2,128)(2,1)} copy(bf16[2,64,2,3072]{1,3,2,0:T(8,128)(2,1)S(1)} %pad_maximum_fusion) | data formatting | bytes 3145728 | tf_op jit(solution)/shard_map/stack | solution.py:112
  (13 shorter events, 0.1 us)
Async XLA Ops:
  4.4 27.8 %all-to-all-start = ((bf16[2,1,4,12288]{3,0,1,2:T(2,128)(2,1)}), bf16[2,1,4,12288]{3,0,1,2:T(2,128)(2,1)S(1)}, u32[]{:S(2)}, u32[]{:S(2)}) async-start(bf16[2,1,4,12288]{3,0,1,2:T(2,128)(2,1)} %copy.220), calls=%async_computation | async-start | bytes 393216 | tf_op jit(solution)/shard_map/all_to_all | solution.py:73
  38.1 8.2 %all-to-all-start.1 = ((bf16[4,2,2,1,3072]{4,2,3,1,0:T(2,128)(2,1)}), bf16[4,2,2,1,3072]{4,2,3,1,0:T(2,128)(2,1)S(1)}, u32[]{:S(2)}, u32[]{:S(2)}) async-start(bf16[4,2,2,1,3072]{4,2,3,1,0:T(2,128)(2,1)} %maximum_bitcast_fusion), calls=%async_computation.1 | async-start | bytes 196608 | tf_op jit(solution)/shard_map/all_to_all | solution.py:78
  81.3 20.0 %slice-start = ((s8[6291456]{0:T(1024)(128)(4,1)}), s8[2097152]{0:T(1024)(128)(4,1)S(1)}, s32[]{:S(2)}) async-start(s8[6291456]{0:T(1024)(128)(4,1)} %bitcast.152), calls=%async_computation.2 | async-start | bytes 4194304
  92.0 9.2 %slice-start.1 = ((s8[6291456]{0:T(1024)(128)(4,1)}), s8[4194304]{0:T(1024)(128)(4,1)S(1)}, s32[]{:S(2)}) async-start(s8[6291456]{0:T(1024)(128)(4,1)} %bitcast.152), calls=%async_computation.3 | async-start | bytes 8388608
  106.7 8.2 %copy-start.1 = (bf16[1,64,16,16]{3,2,1,0:T(8,128)(2,1)S(1)}, bf16[1,64,16,16]{3,2,1,0:T(8,128)(2,1)}, u32[]{:S(2)}) copy-start(bf16[1,64,16,16]{3,2,1,0:T(8,128)(2,1)} %copy.262) | copy-start | bytes 98308
  125.8 9.7 %copy-start = (bf16[64,2,12,16,16]{4,3,2,1,0:T(8,128)(2,1)S(1)}, bf16[64,2,12,16,16]{4,3,2,1,0:T(8,128)(2,1)}, u32[]{:S(2)}) copy-start(bf16[64,2,12,16,16]{4,3,2,1,0:T(8,128)(2,1)} %subtract_convert_fusion) | copy-start | bytes 2359300
  184.2 10.9 %copy-start.2 = (f32[64,2,16,16]{0,3,2,1:T(8,128)S(1)}, f32[64,2,16,16]{0,3,2,1:T(8,128)}, u32[]{:S(2)}) copy-start(f32[64,2,16,16]{0,3,2,1:T(8,128)} %broadcast_multiply_fusion) | copy-start | bytes 393220
